TPU v7x, 32 devices: a whole 2x2x4 slice. The times are simulated.
32 devices in a mesh: aa: 8 (over z, x), ba: 4 (over y, core).
Axes of the slice: x: 2, y: 2, z: 4, core: 2. Of those that a mesh axis runs over, the one named last changes fastest.
Arguments:
- features_a: bfloat16 [16, 32, 256], P('aa', 'ba'), may hold values from -9 to 9
- features_b: bfloat16 [16, 128, 256], P('ba', 'aa'), may hold values from -9 to 9
- conv_in: float32 [8, 3, 3, 3, 3], replicated, may hold values from -0.625 to 0.625
- bias_in: float32 [8], replicated, may hold values from -1 to 1
- conv_out: float32 [8, 3, 3, 3, 3], replicated, may hold values from -0.25 to 0.25
Outputs:
- log_mutual: float32 [16, 32, 16, 128], P('aa', None, 'ba')
- warped: float32 [16, 32, 256], P('aa', 'ba')
All inputs are finite; a program needn't handle non-finite values.
Results may differ from a plain program's by a relative error of at most 0.0035.
Values may be sent and summed in bfloat16 or wider, within the bound.
No kernel may reach another device: no remote copies, remote signals or barrier semaphores. Data moves between devices by JAX's collectives and lax.ppermute only.
A program may use at most 64 MiB of HBM per device.

v0:
```python
import math
import jax
import jax.numpy as jnp
from jax import lax
from jax.sharding import PartitionSpec as P


def padded_2(cells, sides, width):
    for axis, dim in sides:
        count = lax.axis_size(axis)
        ends = count - 1
        head = lax.slice_in_dim(cells, 0, width, axis=dim)
        tail = lax.slice_in_dim(cells, cells.shape[dim] - width, cells.shape[dim], axis=dim)
        cells = jnp.concatenate(
            [
                lax.ppermute(tail, axis, [(i, (i + 1) % count) for i in range(ends)]),
                cells,
                lax.ppermute(head, axis, [((i + 1) % count, i) for i in range(ends)]),
            ],
            axis=dim,
        )
    return cells


def tap_offsets():
    return [
        (step_one, step_two, step_three, step_four)
        for step_one in range(3)
        for step_two in range(3)
        for step_three in range(3)
        for step_four in range(3)
    ]


def spread_taps(padded, kernel, bias_in):
    extent = [size_here - 2 for size_here in padded.shape]
    result = jnp.zeros([kernel.shape[0]] + extent, jnp.float32)
    for offsets in tap_offsets():
        window = padded[
            offsets[0] : offsets[0] + extent[0],
            offsets[1] : offsets[1] + extent[1],
            offsets[2] : offsets[2] + extent[2],
            offsets[3] : offsets[3] + extent[3],
        ]
        result = (
            result
            + kernel[:, offsets[0], offsets[1], offsets[2], offsets[3]].reshape(-1, 1, 1, 1, 1)
            * window[None]
        )
    return jax.nn.relu(result + bias_in.reshape(-1, 1, 1, 1, 1))


def reduce_taps(padded, kernel):
    extent = [size_here - 2 for size_here in padded.shape[1:]]
    result = jnp.zeros(extent, jnp.float32)
    for offsets in tap_offsets():
        window = padded[
            :,
            offsets[0] : offsets[0] + extent[0],
            offsets[1] : offsets[1] + extent[1],
            offsets[2] : offsets[2] + extent[2],
            offsets[3] : offsets[3] + extent[3],
        ]
        result = result + jnp.sum(
            kernel[:, offsets[0], offsets[1], offsets[2], offsets[3]].reshape(-1, 1, 1, 1, 1)
            * window,
            axis=0,
        )
    return result


def dual_norms(values):
    top_a = lax.pmax(jnp.max(values, axis=(0, 1)), "aa")
    top_b = lax.pmax(jnp.max(values, axis=(2, 3)), "ba")
    mass_a = lax.psum(jnp.sum(jnp.exp(values - top_a), axis=(0, 1)), "aa")
    mass_b = lax.psum(jnp.sum(jnp.exp(values - top_b[:, :, None, None]), axis=(2, 3)), "ba")
    norm_a = top_a + jnp.log(mass_a)
    norm_b = top_b + jnp.log(mass_b)
    return (norm_a, norm_b[:, :, None, None])


def local(features_a, features_b, conv_in, bias_in, conv_out):
    channels = features_a.shape[2]
    rows_a = lax.all_gather(features_a, "ba", axis=1, tiled=True)
    rows_b = lax.all_gather(features_b, "aa", axis=1, tiled=True)
    height_a = rows_a.shape[0]
    width_a = rows_a.shape[1]
    height_b = rows_b.shape[0]
    width_b = rows_b.shape[1]
    grid_a = height_a * lax.axis_size("aa")
    grid_b = height_b * lax.axis_size("ba")
    offset = math.log(grid_a * width_a * grid_b * width_b)
    scores = jnp.einsum(
        "xyc,uvc->xyuv", rows_a, rows_b, preferred_element_type=jnp.float32
    ) / math.sqrt(channels)
    norm_a, norm_b = dual_norms(scores)
    matched = jax.nn.softplus(2.0 * scores - norm_a - norm_b + offset)
    rim = padded_2(matched, (("aa", 0), ("ba", 2)), 1)
    hidden = spread_taps(jnp.pad(rim, ((0, 0), (1, 1), (0, 0), (1, 1))), conv_in, bias_in)
    rim_hidden = padded_2(hidden, (("aa", 1), ("ba", 3)), 1)
    filtered = reduce_taps(jnp.pad(rim_hidden, ((0, 0), (0, 0), (1, 1), (0, 0), (1, 1))), conv_out)
    refined = scores + jax.nn.relu(filtered)
    norm_a2, norm_b2 = dual_norms(refined)
    log_mutual = 2.0 * refined - norm_a2 - norm_b2 + offset
    weights = jnp.exp(refined - norm_b2).astype(jnp.bfloat16)
    transfer_terms = jnp.einsum(
        "xyuv,uvc->xyc", weights, rows_b, preferred_element_type=jnp.float32
    )
    warped = lax.psum_scatter(transfer_terms, "ba", scatter_dimension=1, tiled=True)
    return (log_mutual, warped)


def solution(mesh):
    placed = (P("aa", "ba", None), P("ba", "aa", None), P(), P(), P())
    return jax.shard_map(
        local,
        mesh=mesh,
        in_specs=placed,
        out_specs=(P("aa", None, "ba", None), P("aa", "ba", None)),
        check_vma=False,
    )
```

profile of v0, /device:TPU:0, one launch (start us, length us, event | category | flops | bytes accessed | tf_op | source)
XLA Modules:
  0.0 315.4 jit_solution(11921888077074273181)
XLA Ops:
  7.2 32.8 %all_gather.7 = bf16[4,128,256]{2,1,0:T(8,128)(2,1)S(1)} all-gather(bf16[4,16,256]{2,1,0:T(8,128)(2,1)} %param.6), channel_id=1, replica_groups=mesh['aa'=8,'ba'=4] {'aa'}, dimensions={1}, use_global_device_ids=true | all-gather | bytes 294912 | tf_op jit(solution)/shard_map/all_gather | solution.py:85
  40.0 5.4 %all_gather.6 = bf16[2,32,256]{2,1,0:T(8,128)(2,1)S(1)} all-gather(bf16[2,8,256]{2,1,0:T(8,128)(2,1)} %param.5), channel_id=1, replica_groups=mesh['aa'=8,'ba'=4] {'ba'}, dimensions={1}, use_global_device_ids=true | all-gather | bytes 40960 | tf_op jit(solution)/shard_map/all_gather | solution.py:84
  45.6 21.4 %pmax.28 = f32[4,128]{1,0:T(4,128)S(1)} all-reduce(f32[4,128]{1,0:T(4,128)S(1)} %get-tuple-element.348), channel_id=1, replica_groups=mesh['aa'=8,'ba'=4] {'aa'}, use_global_device_ids=true, to_apply=%region_1.0 | all-reduce | flops 512 | bytes 4096 | tf_op jit(solution)/shard_map/pmax | solution.py:73
  67.1 5.7 %pmax.29 = f32[2,32]{1,0:T(2,128)S(1)} all-reduce(f32[2,32]{1,0:T(2,128)S(1)} %get-tuple-element.92), channel_id=1, replica_groups=mesh['aa'=8,'ba'=4] {'ba'}, use_global_device_ids=true, to_apply=%region_5.0 | all-reduce | flops 64 | bytes 512 | tf_op jit(solution)/shard_map/pmax | solution.py:74
  72.9 6.6 %psum.29 = f32[2,32]{1,0:T(2,128)S(1)} all-reduce(f32[2,32]{1,0:T(2,128)S(1)} %exponential_reduce_fusion.2), channel_id=1, replica_groups=mesh['aa'=8,'ba'=4] {'ba'}, use_global_device_ids=true, to_apply=%region_7.0 | all-reduce | flops 64 | bytes 512 | tf_op jit(solution)/shard_map/psum | solution.py:76
  79.6 17.1 %psum.28 = f32[4,128]{1,0:T(4,128)S(1)} all-reduce(f32[4,128]{1,0:T(4,128)S(1)} %get-tuple-element.91), channel_id=1, replica_groups=mesh['aa'=8,'ba'=4] {'aa'}, use_global_device_ids=true, to_apply=%region_3.0 | all-reduce | flops 512 | bytes 4096 | tf_op jit(solution)/shard_map/psum | solution.py:75
  96.9 4.0 %collective-permute-start = (f32[1,32,4,128]{3,1,2,0:T(8,128)S(1)}, f32[1,32,4,128]{3,1,2,0:T(8,128)S(1)}, u32[]{:S(2)}, u32[]{:S(2)}) collective-permute-start(f32[1,32,4,128]{3,1,2,0:T(8,128)S(1)} %get-tuple-element.184), channel_id=1, source_target_pairs={{0,4},{4,8},{8,12},{12,16},{16,20},{20,24},{24,28},{1,5},{5,9},{9,... | collective-permute-start | bytes 196616 | tf_op jit(solution)/shard_map/ppermute | solution.py:16
  103.6 1.5 slice_bitcast_fusion.159
  105.2 1.5 slice_bitcast_fusion.158
  110.9 1.8 collective-permute-start.3
  113.0 2.1 collective-permute-done.3
  166.7 12.1 %add_maximum_fusion = f32[8,2,32,4,128]{4,0,3,2,1:T(8,128)S(1)} fusion(f32[8]{0:T(128)} %param.8, f32[2,32,4,128]{3,2,1,0:T(4,128)} %copy.169, f32[8]{0:T(128)} %get-tuple-element.346, f32[2,32,4,128]{3,2,1,0:T(4,128)} %copy.168, f32[8]{0:T(128)} %get-tuple-element.347, f32[2,32,4,128]{3,2,1,0:T(4,128)} %copy.167, f32[8]{0:T(128)S(1)} %get-tuple-element.268, ...), kind=kLoop, calls=%fused_computation.181 | loop fusion | flops 42729472 | bytes 11668032 | tf_op jit(solution)/shard_map/jit(relu)/max | solution.py:50
  178.9 4.6 %collective-permute-start.4 = (f32[8,1,32,4,128]{4,0,3,2,1:T(8,128)S(1)}, f32[8,1,32,4,128]{4,0,3,2,1:T(8,128)S(1)}, u32[]{:S(2)}, u32[]{:S(2)}) collective-permute-start(f32[8,1,32,4,128]{4,0,3,2,1:T(8,128)S(1)} %get-tuple-element.98), channel_id=1, source_target_pairs={{0,4},{4,8},{8,12},{12,16},{16,20},{20,24},{24,28},{1,5},{5,9},{9,... | collective-permute-start | bytes 1572872 | tf_op jit(solution)/shard_map/ppermute | solution.py:16
  187.4 17.6 %collective-permute-done.4 = f32[8,1,32,4,128]{4,0,3,2,1:T(8,128)S(1)} collective-permute-done((f32[8,1,32,4,128]{4,0,3,2,1:T(8,128)S(1)}, f32[8,1,32,4,128]{4,0,3,2,1:T(8,128)S(1)}, u32[]{:S(2)}, u32[]{:S(2)}) %collective-permute-start.4) | collective-permute-done | bytes 524320 | tf_op jit(solution)/shard_map/ppermute | solution.py:16
  205.1 4.0 %collective-permute-start.6 = (f32[8,4,32,1,128]{4,0,3,2,1:T(8,128)S(1)}, f32[8,4,32,1,128]{4,0,3,2,1:T(8,128)S(1)}, u32[]{:S(2)}, u32[]{:S(2)}) collective-permute-start(f32[8,4,32,1,128]{4,0,3,2,1:T(8,128)S(1)} %get-tuple-element.96), channel_id=1, source_target_pairs={{0,1},{1,2},{2,3},{4,5},{5,6},{6,7},{8,9},{9,10},{10,11},{12,13},{... | collective-permute-start | bytes 1572872 | tf_op jit(solution)/shard_map/ppermute | solution.py:16
  213.3 1.7 fusion.71
  215.4 1.7 fusion.74
  217.1 1.7 fusion.67
  218.8 4.0 %select_maximum_fusion = f32[8,4,34,6,130]{4,0,3,2,1:T(8,128)S(1)} fusion(f32[8,4,32,1,128]{4,0,3,2,1:T(8,128)S(1)} %collective-permute-done.7, f32[8,4,32,1,128]{4,0,3,2,1:T(8,128)S(1)} %collective-permute-done.6, f32[8,1,32,4,128]{4,0,3,2,1:T(8,128)S(1)} %collective-permute-done.5, f32[8,2,32,4,128]{4,0,3,2,1:T(8,128)S(1)} %add_maximum_fusion, ...), kind=kLoop, calls=%fused_computation.4 | loop fusion | flops 17821440 | bytes 6540288 | tf_op jit(solution)/shard_map/concatenate | solution.py:14
  222.8 3.2 %fusion.81 = (f32[2,32,4,128]{3,2,1,0:T(4,128)S(1)}, f32[2,32,4,128]{3,2,1,0:T(4,128)S(1)}, f32[2,32,4,128]{3,2,1,0:T(4,128)S(1)}, f32[2,32,4,128]{3,2,1,0:T(4,1...) fusion(f32[8,4,34,6,130]{4,0,3,2,1:T(8,128)S(1)} %select_maximu, ...), kind=kLoop, calls=%fused_computation.173 | loop fusion | flops 4423680 | bytes 10617120 | tf_op jit(solution)/shard_map/reduce_sum | solution.py:64
  226.0 3.2 %fusion.80 = (f32[2,32,4,128]{3,2,1,0:T(4,128)S(1)}, f32[2,32,4,128]{3,2,1,0:T(4,128)S(1)}, f32[2,32,4,128]{3,2,1,0:T(4,128)S(1)}, f32[2,32,4,128]{3,2,1,0:T(4,1...) fusion(f32[8,4,34,6,130]{4,0,3,2,1:T(8,128)S(1)} %select_maximu, ...), kind=kLoop, calls=%fused_computation.171 | loop fusion | flops 4423680 | bytes 10617120 | tf_op jit(solution)/shard_map/reduce_sum | solution.py:64
  229.2 3.3 %fusion.79 = (f32[2,32,4,128]{3,2,1,0:T(4,128)S(1)}, f32[2,32,4,128]{3,2,1,0:T(4,128)S(1)}, f32[2,32,4,128]{3,2,1,0:T(4,128)S(1)}, f32[2,32,4,128]{3,2,1,0:T(4,1...) fusion(f32[8,4,34,6,130]{4,0,3,2,1:T(8,128)S(1)} %select_maximu, ...), kind=kLoop, calls=%fused_computation.169 | loop fusion | flops 4423680 | bytes 10617120 | tf_op jit(solution)/shard_map/reduce_sum | solution.py:64
  232.5 3.6 %fusion.78 = (f32[2,32,4,128]{3,2,1,0:T(4,128)S(1)}, f32[2,32,4,128]{3,2,1,0:T(4,128)S(1)}, f32[2,32,4,128]{3,2,1,0:T(4,128)S(1)}, f32[2,32,4,128]{3,2,1,0:T(4,1...) fusion(f32[8,4,34,6,130]{4,0,3,2,1:T(8,128)S(1)} %select_maximu, ...), kind=kLoop, calls=%fused_computation.167 | loop fusion | flops 4423680 | bytes 10617120 | tf_op jit(solution)/shard_map/reduce_sum | solution.py:64
  236.2 3.2 %fusion.83 = (f32[2,32,4,128]{3,2,1,0:T(4,128)S(1)}, f32[2,32,4,128]{3,2,1,0:T(4,128)S(1)}, f32[2,32,4,128]{3,2,1,0:T(4,128)S(1)}, f32[2,32,4,128]{3,2,1,0:T(4,1...) fusion(f32[8,4,34,6,130]{4,0,3,2,1:T(8,128)S(1)} %select_maximu, ...), kind=kLoop, calls=%fused_computation.177 | loop fusion | flops 4423680 | bytes 10617120 | tf_op jit(solution)/shard_map/reduce_sum | solution.py:64
  239.5 4.1 %fusion.82 = (f32[2,32,4,128]{3,2,1,0:T(4,128)}, f32[2,32,4,128]{3,2,1,0:T(4,128)}, f32[2,32,4,128]{3,2,1,0:T(4,128)}, f32[2,32,4,128]{3,2,1,0:T(4,128)}, f32[2,...) fusion(f32[8,4,34,6,130]{4,0,3,2,1:T(8,128)S(1)} %select_maximu, ...), kind=kLoop, calls=%fused_computation.175 | loop fusion | flops 4423680 | bytes 10617120 | tf_op jit(solution)/shard_map/reduce_sum | solution.py:64
  243.6 4.1 %fusion.84 = (f32[2,32,4,128]{3,2,1,0:T(4,128)}, f32[2,32,4,128]{3,2,1,0:T(4,128)}, f32[2,32,4,128]{3,2,1,0:T(4,128)}, f32[2,32,4,128]{3,2,1,0:T(4,128)}, f32[2,...) fusion(f32[8,4,34,6,130]{4,0,3,2,1:T(8,128)S(1)} %select_maximu, ...), kind=kLoop, calls=%fused_computation.179 | loop fusion | flops 4423680 | bytes 10617120 | tf_op jit(solution)/shard_map/reduce_sum | solution.py:64
  247.7 4.2 %fusion.77 = (f32[2,32,4,128]{3,2,1,0:T(4,128)}, f32[2,32,4,128]{3,2,1,0:T(4,128)}, f32[2,32,4,128]{3,2,1,0:T(4,128)}, f32[2,32,4,128]{3,2,1,0:T(4,128)}, f32[2,...) fusion(f32[8,4,34,6,130]{4,0,3,2,1:T(8,128)S(1)} %select_maximu, ...), kind=kLoop, calls=%fused_computation.165 | loop fusion | flops 4423680 | bytes 10617120 | tf_op jit(solution)/shard_map/reduce_sum | solution.py:64
  251.9 3.1 fusion.95
  255.0 19.3 %pmax.30 = f32[4,128]{1,0:T(4,128)S(1)} all-reduce(f32[4,128]{1,0:T(4,128)S(1)} %get-tuple-element.89), channel_id=1, replica_groups=mesh['aa'=8,'ba'=4] {'aa'}, use_global_device_ids=true, to_apply=%region_90.91 | all-reduce | flops 512 | bytes 4096 | tf_op jit(solution)/shard_map/pmax | solution.py:73
  274.3 7.8 %pmax.31 = f32[2,32]{1,0:T(2,128)S(1)} all-reduce(f32[2,32]{1,0:T(2,128)S(1)} %get-tuple-element.90), channel_id=1, replica_groups=mesh['aa'=8,'ba'=4] {'ba'}, use_global_device_ids=true, to_apply=%region_94.95 | all-reduce | flops 64 | bytes 512 | tf_op jit(solution)/shard_map/pmax | solution.py:74
  282.3 7.2 %psum.31 = f32[2,32]{1,0:T(2,128)S(1)} all-reduce(f32[2,32]{1,0:T(2,128)S(1)} %get-tuple-element.88), channel_id=1, replica_groups=mesh['aa'=8,'ba'=4] {'ba'}, use_global_device_ids=true, to_apply=%region_96.97 | all-reduce | flops 64 | bytes 512 | tf_op jit(solution)/shard_map/psum | solution.py:76
  290.4 17.1 %psum.30 = f32[4,128]{1,0:T(4,128)S(1)} all-reduce(f32[4,128]{1,0:T(4,128)S(1)} %get-tuple-element.87), channel_id=1, replica_groups=mesh['aa'=8,'ba'=4] {'aa'}, use_global_device_ids=true, to_apply=%region_92.93 | all-reduce | flops 512 | bytes 4096 | tf_op jit(solution)/shard_map/psum | solution.py:75
  (151 shorter events, 69.9 us)
Async XLA Ops:
  7.2 301.2 %reduce-scatter.2.cloned.1.call-start = ((), (), s32[]{:S(2)}) async-start(), calls=%async_computation.1 | async-start | bytes 81920 | tf_op jit(solution)/shard_map/reduce_scatter | solution.py:109
  96.9 12.7 %collective-permute-start = (f32[1,32,4,128]{3,1,2,0:T(8,128)S(1)}, f32[1,32,4,128]{3,1,2,0:T(8,128)S(1)}, u32[]{:S(2)}, u32[]{:S(2)}) collective-permute-start(f32[1,32,4,128]{3,1,2,0:T(8,128)S(1)} %get-tuple-element.184), channel_id=1, source_target_pairs={{0,4},{4,8},{8,12},{12,16},{16,20},{20,24},{24,28},{1,5},{5,9},{9,... | collective-permute-start | bytes 196616 | tf_op jit(solution)/shard_map/ppermute | solution.py:16
  100.8 8.8 %collective-permute-start.1 = (f32[1,32,4,128]{3,1,2,0:T(8,128)S(1)}, f32[1,32,4,128]{3,1,2,0:T(8,128)S(1)}, u32[]{:S(2)}, u32[]{:S(2)}) collective-permute-start(f32[1,32,4,128]{3,1,2,0:T(8,128)S(1)} %get-tuple-element.185), channel_id=1, source_target_pairs={{4,0},{8,4},{12,8},{16,12},{20,16},{24,20},{28,24},{5,1},{9,5},{13... | collective-permute-start | bytes 196616 | tf_op jit(solution)/shard_map/ppermute | solution.py:18
  109.6 3.3 %collective-permute-start.2 = (f32[4,32,1,128]{3,1,2,0:T(8,128)S(1)}, f32[4,32,1,128]{3,1,2,0:T(8,128)S(1)}, u32[]{:S(2)}, u32[]{:S(2)}) collective-permute-start(f32[4,32,1,128]{3,1,2,0:T(8,128)S(1)} %get-tuple-element.180), channel_id=1, source_target_pairs={{0,1},{1,2},{2,3},{4,5},{5,6},{6,7},{8,9},{9,10},{10,11},{12,13},{... | collective-permute-start | bytes 196616 | tf_op jit(solution)/shard_map/ppermute | solution.py:16
  110.9 4.2 %collective-permute-start.3 = (f32[4,32,1,128]{3,1,2,0:T(8,128)S(1)}, f32[4,32,1,128]{3,1,2,0:T(8,128)S(1)}, u32[]{:S(2)}, u32[]{:S(2)}) collective-permute-start(f32[4,32,1,128]{3,1,2,0:T(8,128)S(1)} %get-tuple-element.181), channel_id=1, source_target_pairs={{1,0},{2,1},{3,2},{5,4},{6,5},{7,6},{9,8},{10,9},{11,10},{13,12},{... | collective-permute-start | bytes 196616 | tf_op jit(solution)/shard_map/ppermute | solution.py:18
  178.9 26.1 %collective-permute-start.4 = (f32[8,1,32,4,128]{4,0,3,2,1:T(8,128)S(1)}, f32[8,1,32,4,128]{4,0,3,2,1:T(8,128)S(1)}, u32[]{:S(2)}, u32[]{:S(2)}) collective-permute-start(f32[8,1,32,4,128]{4,0,3,2,1:T(8,128)S(1)} %get-tuple-element.98), channel_id=1, source_target_pairs={{0,4},{4,8},{8,12},{12,16},{16,20},{20,24},{24,28},{1,5},{5,9},{9,... | collective-permute-start | bytes 1572872 | tf_op jit(solution)/shard_map/ppermute | solution.py:16
  183.5 21.5 %collective-permute-start.5 = (f32[8,1,32,4,128]{4,0,3,2,1:T(8,128)S(1)}, f32[8,1,32,4,128]{4,0,3,2,1:T(8,128)S(1)}, u32[]{:S(2)}, u32[]{:S(2)}) collective-permute-start(f32[8,1,32,4,128]{4,0,3,2,1:T(8,128)S(1)} %get-tuple-element.99), channel_id=1, source_target_pairs={{4,0},{8,4},{12,8},{16,12},{20,16},{24,20},{28,24},{5,1},{9,5},{13... | collective-permute-start | bytes 1572872 | tf_op jit(solution)/shard_map/ppermute | solution.py:18
  205.1 9.9 %collective-permute-start.6 = (f32[8,4,32,1,128]{4,0,3,2,1:T(8,128)S(1)}, f32[8,4,32,1,128]{4,0,3,2,1:T(8,128)S(1)}, u32[]{:S(2)}, u32[]{:S(2)}) collective-permute-start(f32[8,4,32,1,128]{4,0,3,2,1:T(8,128)S(1)} %get-tuple-element.96), channel_id=1, source_target_pairs={{0,1},{1,2},{2,3},{4,5},{5,6},{6,7},{8,9},{9,10},{10,11},{12,13},{... | collective-permute-start | bytes 1572872 | tf_op jit(solution)/shard_map/ppermute | solution.py:16
  209.1 5.9 %collective-permute-start.7 = (f32[8,4,32,1,128]{4,0,3,2,1:T(8,128)S(1)}, f32[8,4,32,1,128]{4,0,3,2,1:T(8,128)S(1)}, u32[]{:S(2)}, u32[]{:S(2)}) collective-permute-start(f32[8,4,32,1,128]{4,0,3,2,1:T(8,128)S(1)} %get-tuple-element.97), channel_id=1, source_target_pairs={{1,0},{2,1},{3,2},{5,4},{6,5},{7,6},{9,8},{10,9},{11,10},{13,12},{... | collective-permute-start | bytes 1572872 | tf_op jit(solution)/shard_map/ppermute | solution.py:18
  232.5 3.7 %copy-start.3 = (f32[8]{0:T(128)S(1)}, f32[8]{0:T(128)}, u32[]{:S(2)}) copy-start(f32[8]{0:T(128)} %get-tuple-element.263) | copy-start | bytes 100
  236.1 3.4 %copy-start.2 = (f32[8]{0:T(128)S(1)}, f32[8]{0:T(128)}, u32[]{:S(2)}) copy-start(f32[8]{0:T(128)} %get-tuple-element.262) | copy-start | bytes 100
  236.1 3.4 %copy-start.4 = (f32[8]{0:T(128)S(1)}, f32[8]{0:T(128)}, u32[]{:S(2)}) copy-start(f32[8]{0:T(128)} %get-tuple-element.206) | copy-start | bytes 100
  236.1 3.4 %copy-start.5 = (f32[8]{0:T(128)S(1)}, f32[8]{0:T(128)}, u32[]{:S(2)}) copy-start(f32[8]{0:T(128)} %get-tuple-element.207) | copy-start | bytes 100
  236.1 3.4 %copy-start.6 = (f32[8]{0:T(128)S(1)}, f32[8]{0:T(128)}, u32[]{:S(2)}) copy-start(f32[8]{0:T(128)} %get-tuple-element.208) | copy-start | bytes 100
  236.1 3.4 %copy-start.7 = (f32[8]{0:T(128)S(1)}, f32[8]{0:T(128)}, u32[]{:S(2)}) copy-start(f32[8]{0:T(128)} %get-tuple-element.209) | copy-start | bytes 100
  236.1 3.4 %copy-start.8 = (f32[8]{0:T(128)S(1)}, f32[8]{0:T(128)}, u32[]{:S(2)}) copy-start(f32[8]{0:T(128)} %get-tuple-element.210) | copy-start | bytes 100
  236.1 3.4 %copy-start.9 = (f32[8]{0:T(128)S(1)}, f32[8]{0:T(128)}, u32[]{:S(2)}) copy-start(f32[8]{0:T(128)} %get-tuple-element.211) | copy-start | bytes 100
  236.1 3.4 %copy-start.10 = (f32[8]{0:T(128)S(1)}, f32[8]{0:T(128)}, u32[]{:S(2)}) copy-start(f32[8]{0:T(128)} %get-tuple-element.212) | copy-start | bytes 100
  236.1 3.4 %copy-start.11 = (f32[8]{0:T(128)S(1)}, f32[8]{0:T(128)}, u32[]{:S(2)}) copy-start(f32[8]{0:T(128)} %get-tuple-element.213) | copy-start | bytes 100
  239.4 4.2 %copy-start = (f32[8]{0:T(128)S(1)}, f32[8]{0:T(128)}, u32[]{:S(2)}) copy-start(f32[8]{0:T(128)} %get-tuple-element.264) | copy-start | bytes 100
  239.4 4.2 %copy-start.1 = (f32[8]{0:T(128)S(1)}, f32[8]{0:T(128)}, u32[]{:S(2)}) copy-start(f32[8]{0:T(128)} %get-tuple-element.266) | copy-start | bytes 100
Sparse Core Ops, SparseCore 0:
  290.5 16.0 reduce-scatter.1
where the time goes:
time: 319 us; the launch traced here: 315 us
  blocking collectives  140 us (44%)
  local copies, waits for them, and re-layouts  65 us (20%)
  other arithmetic  54.8 us (17%)
  waiting for transfers between devices  19.8 us (6%)
  starting transfers between devices  19.6 us (6%)
  between operations  14.8 us (5%)
    slice x85, local copies, waits for them, and re-layouts, spread_taps(): padded[offsets[0]:offsets[0] + extent[0], offsets[1]:offsets[1] + extent[...  51.2 us
    pmax x2, blocking collectives, dual_norms(): top_a = lax.pmax(jnp.max(values, axis=(0, 1)), 'aa')  40.7 us
    psum x2, blocking collectives, dual_norms(): mass_a = lax.psum(jnp.sum(jnp.exp(values - top_a), axis=(0, 1)), 'aa')  34.3 us
    reduce_sum x11, other arithmetic, reduce_taps(): jnp.sum(kernel[:, offsets[0], offsets[1], offsets[2], offsets[3]].reshape...  33.9 us
    all_gather x1, blocking collectives, local(): rows_b = lax.all_gather(features_b, 'aa', axis=1, tiled=True)  32.8 us
    ppermute x4, waiting for transfers between devices, padded_2(): lax.ppermute(tail, axis, [(i, (i + 1) % count) for i in range(ends)])  17.6 us
    psum x2, blocking collectives, dual_norms(): lax.psum(jnp.sum(jnp.exp(values - top_b[:, :, None, None]), axis=(2, 3)),...  13.9 us
    ppermute x4, starting transfers between devices, padded_2(): lax.ppermute(tail, axis, [(i, (i + 1) % count) for i in range(ends)])  13.8 us
  transfers between devices with their start and end apart: 9, of which 2 were waited for; matrix products, arithmetic and copies ran while one was open for 5% of the time, Pallas kernels for 0%

commit v1 on v0

--- a/solution.py
+++ b/solution.py
@@ -72,7 +72,12 @@
 def dual_norms(values):
     top_a = lax.pmax(jnp.max(values, axis=(0, 1)), "aa")
     top_b = lax.pmax(jnp.max(values, axis=(2, 3)), "ba")
-    mass_a = lax.psum(jnp.sum(jnp.exp(values - top_a), axis=(0, 1)), "aa")
+
+    def _register_weights(frame_in):
+        r2 = jnp.sum(lax.all_gather(frame_in, "aa"), axis=0)
+        return r2
+
+    mass_a = _register_weights(jnp.sum(jnp.exp(values - top_a), axis=(0, 1)))
     mass_b = lax.psum(jnp.sum(jnp.exp(values - top_b[:, :, None, None]), axis=(2, 3)), "ba")
     norm_a = top_a + jnp.log(mass_a)
     norm_b = top_b + jnp.log(mass_b)

time: 319 us -> 335 us (1.050)
  blocking collectives: 140 us -> 160 us
    all_gather x0 -> x2, blocking collectives: none -> 52.2 us  [_register_weights(): r2 = jnp.sum(lax.all_gather(frame_in, 'aa'), axis=0)]
    psum x2 -> x0, blocking collectives: 34.3 us -> none  [dual_norms(): mass_a = lax.psum(jnp.sum(jnp.exp(values - top_a), axis=(0, 1)), 'aa')]
where the time goes in v1:
time: 335 us; the launch traced here: 332 us
  blocking collectives  160 us (48%)
  local copies, waits for them, and re-layouts  65 us (19%)
  other arithmetic  54.7 us (16%)
  waiting for transfers between devices  19.8 us (6%)
  starting transfers between devices  17.2 us (5%)
  between operations  14.8 us (4%)
    all_gather x2, blocking collectives, _register_weights(): r2 = jnp.sum(lax.all_gather(frame_in, 'aa'), axis=0)  52.2 us
    slice x85, local copies, waits for them, and re-layouts, spread_taps(): padded[offsets[0]:offsets[0] + extent[0], offsets[1]:offsets[1] + extent[...  51.2 us
    pmax x2, blocking collectives, dual_norms(): top_a = lax.pmax(jnp.max(values, axis=(0, 1)), 'aa')  41.8 us
    reduce_sum x11, other arithmetic, reduce_taps(): jnp.sum(kernel[:, offsets[0], offsets[1], offsets[2], offsets[3]].reshape...  33.9 us
    all_gather x1, blocking collectives, local(): rows_b = lax.all_gather(features_b, 'aa', axis=1, tiled=True)  32.8 us
    ppermute x4, waiting for transfers between devices, padded_2(): lax.ppermute(tail, axis, [(i, (i + 1) % count) for i in range(ends)])  17.6 us
    psum x2, blocking collectives, dual_norms(): lax.psum(jnp.sum(jnp.exp(values - top_b[:, :, None, None]), axis=(2, 3)),...  13.9 us
    pmax x2, blocking collectives, dual_norms(): top_b = lax.pmax(jnp.max(values, axis=(2, 3)), 'ba')  13.5 us
  transfers between devices with their start and end apart: 9, of which 2 were waited for; matrix products, arithmetic and copies ran while one was open for 5% of the time, Pallas kernels for 0%

profile of v1, /device:TPU:0, one launch (start us, length us, event | category | flops | bytes accessed | tf_op | source)
XLA Modules:
  0.0 332.2 jit_solution(8828996631137590380)
XLA Ops:
  7.2 32.8 %all_gather.19 = bf16[4,128,256]{2,1,0:T(8,128)(2,1)S(1)} all-gather(bf16[4,16,256]{2,1,0:T(8,128)(2,1)} %param.6), channel_id=1, replica_groups=mesh['aa'=8,'ba'=4] {'aa'}, dimensions={1}, use_global_device_ids=true | all-gather | bytes 294912 | tf_op jit(solution)/shard_map/all_gather | solution.py:90
  40.0 5.4 %all_gather.18 = bf16[2,32,256]{2,1,0:T(8,128)(2,1)S(1)} all-gather(bf16[2,8,256]{2,1,0:T(8,128)(2,1)} %param.5), channel_id=1, replica_groups=mesh['aa'=8,'ba'=4] {'ba'}, dimensions={1}, use_global_device_ids=true | all-gather | bytes 40960 | tf_op jit(solution)/shard_map/all_gather | solution.py:89
  45.6 21.4 %pmax.28 = f32[4,128]{1,0:T(4,128)S(1)} all-reduce(f32[4,128]{1,0:T(4,128)S(1)} %get-tuple-element.350), channel_id=1, replica_groups=mesh['aa'=8,'ba'=4] {'aa'}, use_global_device_ids=true, to_apply=%region_1.0 | all-reduce | flops 512 | bytes 4096 | tf_op jit(solution)/shard_map/pmax | solution.py:73
  67.1 5.7 %pmax.29 = f32[2,32]{1,0:T(2,128)S(1)} all-reduce(f32[2,32]{1,0:T(2,128)S(1)} %get-tuple-element.94), channel_id=1, replica_groups=mesh['aa'=8,'ba'=4] {'ba'}, use_global_device_ids=true, to_apply=%region_5.0 | all-reduce | flops 64 | bytes 512 | tf_op jit(solution)/shard_map/pmax | solution.py:74
  72.9 6.6 %psum.14 = f32[2,32]{1,0:T(2,128)S(1)} all-reduce(f32[2,32]{1,0:T(2,128)S(1)} %exponential_reduce_fusion.2), channel_id=1, replica_groups=mesh['aa'=8,'ba'=4] {'ba'}, use_global_device_ids=true, to_apply=%region_7.0 | all-reduce | flops 64 | bytes 512 | tf_op jit(solution)/shard_map/psum | solution.py:81
  79.5 26.1 %all-gather.2 = f32[8,4,128]{2,1,0:T(4,128)S(1)} all-gather(f32[1,4,128]{2,1,0:T(4,128)S(1)} %bitcast.344), channel_id=2, replica_groups=mesh['aa'=8,'ba'=4] {'aa'}, dimensions={0}, use_global_device_ids=true | all-gather | bytes 18432 | tf_op jit(solution)/shard_map/all_gather | solution.py:77
  110.0 1.5 slice_bitcast_fusion.159
  111.5 1.5 slice_bitcast_fusion.158
  113.0 1.5 slice_bitcast_fusion.157
  117.3 1.8 collective-permute-start.3
  119.3 2.2 collective-permute-done.3
  173.1 12.0 %add_maximum_fusion = f32[8,2,32,4,128]{4,0,3,2,1:T(8,128)S(1)} fusion(f32[8]{0:T(128)} %param.8, f32[2,32,4,128]{3,2,1,0:T(4,128)} %copy.251, f32[8]{0:T(128)} %get-tuple-element.348, f32[2,32,4,128]{3,2,1,0:T(4,128)} %copy.250, f32[8]{0:T(128)} %get-tuple-element.349, f32[2,32,4,128]{3,2,1,0:T(4,128)} %copy.249, f32[8]{0:T(128)S(1)} %get-tuple-element.270, ...), kind=kLoop, calls=%fused_computation.181 | loop fusion | flops 42729472 | bytes 11668032 | tf_op jit(solution)/shard_map/jit(relu)/max | solution.py:50
  185.2 4.9 %collective-permute-start.4 = (f32[8,1,32,4,128]{4,0,3,2,1:T(8,128)S(1)}, f32[8,1,32,4,128]{4,0,3,2,1:T(8,128)S(1)}, u32[]{:S(2)}, u32[]{:S(2)}) collective-permute-start(f32[8,1,32,4,128]{4,0,3,2,1:T(8,128)S(1)} %get-tuple-element.100), channel_id=1, source_target_pairs={{0,4},{4,8},{8,12},{12,16},{16,20},{20,24},{24,28},{1,5},{5,9},{9,... | collective-permute-start | bytes 1572872 | tf_op jit(solution)/shard_map/ppermute | solution.py:16
  194.0 17.6 %collective-permute-done.4 = f32[8,1,32,4,128]{4,0,3,2,1:T(8,128)S(1)} collective-permute-done((f32[8,1,32,4,128]{4,0,3,2,1:T(8,128)S(1)}, f32[8,1,32,4,128]{4,0,3,2,1:T(8,128)S(1)}, u32[]{:S(2)}, u32[]{:S(2)}) %collective-permute-start.4) | collective-permute-done | bytes 524320 | tf_op jit(solution)/shard_map/ppermute | solution.py:16
  211.7 4.0 %collective-permute-start.6 = (f32[8,4,32,1,128]{4,0,3,2,1:T(8,128)S(1)}, f32[8,4,32,1,128]{4,0,3,2,1:T(8,128)S(1)}, u32[]{:S(2)}, u32[]{:S(2)}) collective-permute-start(f32[8,4,32,1,128]{4,0,3,2,1:T(8,128)S(1)} %get-tuple-element.98), channel_id=1, source_target_pairs={{0,1},{1,2},{2,3},{4,5},{5,6},{6,7},{8,9},{9,10},{10,11},{12,13},{... | collective-permute-start | bytes 1572872 | tf_op jit(solution)/shard_map/ppermute | solution.py:16
  219.9 1.7 fusion.71
  222.1 1.7 fusion.74
  223.8 1.7 fusion.67
  225.4 4.0 %select_maximum_fusion = f32[8,4,34,6,130]{4,0,3,2,1:T(8,128)S(1)} fusion(f32[8,4,32,1,128]{4,0,3,2,1:T(8,128)S(1)} %collective-permute-done.7, f32[8,4,32,1,128]{4,0,3,2,1:T(8,128)S(1)} %collective-permute-done.6, f32[8,1,32,4,128]{4,0,3,2,1:T(8,128)S(1)} %collective-permute-done.5, f32[8,2,32,4,128]{4,0,3,2,1:T(8,128)S(1)} %add_maximum_fusion, ...), kind=kLoop, calls=%fused_computation.4 | loop fusion | flops 17821440 | bytes 6540288 | tf_op jit(solution)/shard_map/concatenate | solution.py:14
  229.4 3.2 fusion.81
  232.6 3.2 fusion.80
  235.8 3.3 fusion.79
  239.1 3.6 %fusion.78 = (f32[2,32,4,128]{3,2,1,0:T(4,128)S(1)}, f32[2,32,4,128]{3,2,1,0:T(4,128)S(1)}, f32[2,32,4,128]{3,2,1,0:T(4,128)S(1)}, f32[2,32,4,128]{3,2,1,0:T(4,1...) fusion(f32[8,4,34,6,130]{4,0,3,2,1:T(8,128)S(1)} %select_maximu, ...), kind=kLoop, calls=%fused_computation.167 | loop fusion | flops 4423680 | bytes 10617120 | tf_op jit(solution)/shard_map/reduce_sum | solution.py:64
  242.8 3.2 fusion.83
  246.1 4.1 %fusion.82 = (f32[2,32,4,128]{3,2,1,0:T(4,128)}, f32[2,32,4,128]{3,2,1,0:T(4,128)}, f32[2,32,4,128]{3,2,1,0:T(4,128)}, f32[2,32,4,128]{3,2,1,0:T(4,128)}, f32[2,...) fusion(f32[8,4,34,6,130]{4,0,3,2,1:T(8,128)S(1)} %select_maximu, ...), kind=kLoop, calls=%fused_computation.175 | loop fusion | flops 4423680 | bytes 10617120 | tf_op jit(solution)/shard_map/reduce_sum | solution.py:64
  250.2 4.1 %fusion.84 = (f32[2,32,4,128]{3,2,1,0:T(4,128)}, f32[2,32,4,128]{3,2,1,0:T(4,128)}, f32[2,32,4,128]{3,2,1,0:T(4,128)}, f32[2,32,4,128]{3,2,1,0:T(4,128)}, f32[2,...) fusion(f32[8,4,34,6,130]{4,0,3,2,1:T(8,128)S(1)} %select_maximu, ...), kind=kLoop, calls=%fused_computation.179 | loop fusion | flops 4423680 | bytes 10617120 | tf_op jit(solution)/shard_map/reduce_sum | solution.py:64
  254.3 4.2 %fusion.77 = (f32[2,32,4,128]{3,2,1,0:T(4,128)}, f32[2,32,4,128]{3,2,1,0:T(4,128)}, f32[2,32,4,128]{3,2,1,0:T(4,128)}, f32[2,32,4,128]{3,2,1,0:T(4,128)}, f32[2,...) fusion(f32[8,4,34,6,130]{4,0,3,2,1:T(8,128)S(1)} %select_maximu, ...), kind=kLoop, calls=%fused_computation.165 | loop fusion | flops 4423680 | bytes 10617120 | tf_op jit(solution)/shard_map/reduce_sum | solution.py:64
  258.5 3.1 fusion.95
  261.6 20.4 %pmax.30 = f32[4,128]{1,0:T(4,128)S(1)} all-reduce(f32[4,128]{1,0:T(4,128)S(1)} %get-tuple-element.91), channel_id=1, replica_groups=mesh['aa'=8,'ba'=4] {'aa'}, use_global_device_ids=true, to_apply=%region_90.91 | all-reduce | flops 512 | bytes 4096 | tf_op jit(solution)/shard_map/pmax | solution.py:73
  282.0 7.8 %pmax.31 = f32[2,32]{1,0:T(2,128)S(1)} all-reduce(f32[2,32]{1,0:T(2,128)S(1)} %get-tuple-element.92), channel_id=1, replica_groups=mesh['aa'=8,'ba'=4] {'ba'}, use_global_device_ids=true, to_apply=%region_94.95 | all-reduce | flops 64 | bytes 512 | tf_op jit(solution)/shard_map/pmax | solution.py:74
  290.0 7.2 %psum.15 = f32[2,32]{1,0:T(2,128)S(1)} all-reduce(f32[2,32]{1,0:T(2,128)S(1)} %get-tuple-element.90), channel_id=1, replica_groups=mesh['aa'=8,'ba'=4] {'ba'}, use_global_device_ids=true, to_apply=%region_96.97 | all-reduce | flops 64 | bytes 512 | tf_op jit(solution)/shard_map/psum | solution.py:81
  298.1 26.1 %all-gather.3 = f32[8,4,128]{2,1,0:T(4,128)S(1)} all-gather(f32[1,4,128]{2,1,0:T(4,128)S(1)} %bitcast.343), channel_id=3, replica_groups=mesh['aa'=8,'ba'=4] {'aa'}, dimensions={0}, use_global_device_ids=true | all-gather | bytes 18432 | tf_op jit(solution)/shard_map/all_gather | solution.py:77
  (153 shorter events, 69.7 us)
Async XLA Ops:
  7.2 318.0 %reduce-scatter.2.cloned.1.call-start = ((), (), s32[]{:S(2)}) async-start(), calls=%async_computation.1 | async-start | bytes 81920 | tf_op jit(solution)/shard_map/reduce_scatter | solution.py:114
  105.9 10.1 %collective-permute-start = (f32[1,32,4,128]{3,1,2,0:T(8,128)S(1)}, f32[1,32,4,128]{3,1,2,0:T(8,128)S(1)}, u32[]{:S(2)}, u32[]{:S(2)}) collective-permute-start(f32[1,32,4,128]{3,1,2,0:T(8,128)S(1)} %get-tuple-element.186), channel_id=1, source_target_pairs={{0,4},{4,8},{8,12},{12,16},{16,20},{20,24},{24,28},{1,5},{5,9},{9,... | collective-permute-start | bytes 196616 | tf_op jit(solution)/shard_map/ppermute | solution.py:16
  107.2 8.8 %collective-permute-start.1 = (f32[1,32,4,128]{3,1,2,0:T(8,128)S(1)}, f32[1,32,4,128]{3,1,2,0:T(8,128)S(1)}, u32[]{:S(2)}, u32[]{:S(2)}) collective-permute-start(f32[1,32,4,128]{3,1,2,0:T(8,128)S(1)} %get-tuple-element.187), channel_id=1, source_target_pairs={{4,0},{8,4},{12,8},{16,12},{20,16},{24,20},{28,24},{5,1},{9,5},{13... | collective-permute-start | bytes 196616 | tf_op jit(solution)/shard_map/ppermute | solution.py:18
  116.0 3.3 %collective-permute-start.2 = (f32[4,32,1,128]{3,1,2,0:T(8,128)S(1)}, f32[4,32,1,128]{3,1,2,0:T(8,128)S(1)}, u32[]{:S(2)}, u32[]{:S(2)}) collective-permute-start(f32[4,32,1,128]{3,1,2,0:T(8,128)S(1)} %get-tuple-element.182), channel_id=1, source_target_pairs={{0,1},{1,2},{2,3},{4,5},{5,6},{6,7},{8,9},{9,10},{10,11},{12,13},{... | collective-permute-start | bytes 196616 | tf_op jit(solution)/shard_map/ppermute | solution.py:16
  117.3 4.2 %collective-permute-start.3 = (f32[4,32,1,128]{3,1,2,0:T(8,128)S(1)}, f32[4,32,1,128]{3,1,2,0:T(8,128)S(1)}, u32[]{:S(2)}, u32[]{:S(2)}) collective-permute-start(f32[4,32,1,128]{3,1,2,0:T(8,128)S(1)} %get-tuple-element.183), channel_id=1, source_target_pairs={{1,0},{2,1},{3,2},{5,4},{6,5},{7,6},{9,8},{10,9},{11,10},{13,12},{... | collective-permute-start | bytes 196616 | tf_op jit(solution)/shard_map/ppermute | solution.py:18
  185.2 26.4 %collective-permute-start.4 = (f32[8,1,32,4,128]{4,0,3,2,1:T(8,128)S(1)}, f32[8,1,32,4,128]{4,0,3,2,1:T(8,128)S(1)}, u32[]{:S(2)}, u32[]{:S(2)}) collective-permute-start(f32[8,1,32,4,128]{4,0,3,2,1:T(8,128)S(1)} %get-tuple-element.100), channel_id=1, source_target_pairs={{0,4},{4,8},{8,12},{12,16},{16,20},{20,24},{24,28},{1,5},{5,9},{9,... | collective-permute-start | bytes 1572872 | tf_op jit(solution)/shard_map/ppermute | solution.py:16
  190.1 21.5 %collective-permute-start.5 = (f32[8,1,32,4,128]{4,0,3,2,1:T(8,128)S(1)}, f32[8,1,32,4,128]{4,0,3,2,1:T(8,128)S(1)}, u32[]{:S(2)}, u32[]{:S(2)}) collective-permute-start(f32[8,1,32,4,128]{4,0,3,2,1:T(8,128)S(1)} %get-tuple-element.101), channel_id=1, source_target_pairs={{4,0},{8,4},{12,8},{16,12},{20,16},{24,20},{28,24},{5,1},{9,5},{13... | collective-permute-start | bytes 1572872 | tf_op jit(solution)/shard_map/ppermute | solution.py:18
  211.7 9.9 %collective-permute-start.6 = (f32[8,4,32,1,128]{4,0,3,2,1:T(8,128)S(1)}, f32[8,4,32,1,128]{4,0,3,2,1:T(8,128)S(1)}, u32[]{:S(2)}, u32[]{:S(2)}) collective-permute-start(f32[8,4,32,1,128]{4,0,3,2,1:T(8,128)S(1)} %get-tuple-element.98), channel_id=1, source_target_pairs={{0,1},{1,2},{2,3},{4,5},{5,6},{6,7},{8,9},{9,10},{10,11},{12,13},{... | collective-permute-start | bytes 1572872 | tf_op jit(solution)/shard_map/ppermute | solution.py:16
  215.7 5.9 %collective-permute-start.7 = (f32[8,4,32,1,128]{4,0,3,2,1:T(8,128)S(1)}, f32[8,4,32,1,128]{4,0,3,2,1:T(8,128)S(1)}, u32[]{:S(2)}, u32[]{:S(2)}) collective-permute-start(f32[8,4,32,1,128]{4,0,3,2,1:T(8,128)S(1)} %get-tuple-element.99), channel_id=1, source_target_pairs={{1,0},{2,1},{3,2},{5,4},{6,5},{7,6},{9,8},{10,9},{11,10},{13,12},{... | collective-permute-start | bytes 1572872 | tf_op jit(solution)/shard_map/ppermute | solution.py:18
  239.1 3.7 %copy-start.3 = (f32[8]{0:T(128)S(1)}, f32[8]{0:T(128)}, u32[]{:S(2)}) copy-start(f32[8]{0:T(128)} %get-tuple-element.265) | copy-start | bytes 100
  242.7 3.4 %copy-start.2 = (f32[8]{0:T(128)S(1)}, f32[8]{0:T(128)}, u32[]{:S(2)}) copy-start(f32[8]{0:T(128)} %get-tuple-element.264) | copy-start | bytes 100
  242.7 3.4 %copy-start.4 = (f32[8]{0:T(128)S(1)}, f32[8]{0:T(128)}, u32[]{:S(2)}) copy-start(f32[8]{0:T(128)} %get-tuple-element.208) | copy-start | bytes 100
  242.7 3.4 %copy-start.5 = (f32[8]{0:T(128)S(1)}, f32[8]{0:T(128)}, u32[]{:S(2)}) copy-start(f32[8]{0:T(128)} %get-tuple-element.209) | copy-start | bytes 100
  242.7 3.4 %copy-start.6 = (f32[8]{0:T(128)S(1)}, f32[8]{0:T(128)}, u32[]{:S(2)}) copy-start(f32[8]{0:T(128)} %get-tuple-element.210) | copy-start | bytes 100
  242.7 3.4 %copy-start.7 = (f32[8]{0:T(128)S(1)}, f32[8]{0:T(128)}, u32[]{:S(2)}) copy-start(f32[8]{0:T(128)} %get-tuple-element.211) | copy-start | bytes 100
  242.7 3.4 %copy-start.8 = (f32[8]{0:T(128)S(1)}, f32[8]{0:T(128)}, u32[]{:S(2)}) copy-start(f32[8]{0:T(128)} %get-tuple-element.212) | copy-start | bytes 100
  242.7 3.4 %copy-start.9 = (f32[8]{0:T(128)S(1)}, f32[8]{0:T(128)}, u32[]{:S(2)}) copy-start(f32[8]{0:T(128)} %get-tuple-element.213) | copy-start | bytes 100
  242.7 3.4 %copy-start.10 = (f32[8]{0:T(128)S(1)}, f32[8]{0:T(128)}, u32[]{:S(2)}) copy-start(f32[8]{0:T(128)} %get-tuple-element.214) | copy-start | bytes 100
  242.8 3.4 %copy-start.11 = (f32[8]{0:T(128)S(1)}, f32[8]{0:T(128)}, u32[]{:S(2)}) copy-start(f32[8]{0:T(128)} %get-tuple-element.215) | copy-start | bytes 100
  246.0 4.2 %copy-start = (f32[8]{0:T(128)S(1)}, f32[8]{0:T(128)}, u32[]{:S(2)}) copy-start(f32[8]{0:T(128)} %get-tuple-element.266) | copy-start | bytes 100
  246.0 4.2 %copy-start.1 = (f32[8]{0:T(128)S(1)}, f32[8]{0:T(128)}, u32[]{:S(2)}) copy-start(f32[8]{0:T(128)} %get-tuple-element.268) | copy-start | bytes 100
Sparse Core Ops, SparseCore 0:
  298.3 16.0 reduce-scatter.1
